TPU v7x, 256 devices: a whole 4x4x8 slice. The times are simulated.
256 devices in a mesh: orb: 8 (over y, core), aux: 32 (over x, z).
Axes of the slice: x: 4, y: 4, z: 8, core: 2. Of those that a mesh axis runs over, the one named last changes fastest.
Arguments:
- factors: bfloat16 [384, 128, 2048], P('orb', None, 'aux'), may hold values from -6 to 6
- amplitudes: bfloat16 [384, 12, 128, 128], P('orb'), may hold values from -0.15625 to 0.15625
- partners: int32 [384, 12], P('orb'), may hold values from 0 to 383, as said below
- metric_tiles: bfloat16 [128, 128, 128], P('aux'), may hold values from -0.1875 to 0.1875
- tile_pos: int32 [128, 2], P('aux'), may hold values from 0 to 15, as said below
Outputs:
- density: bfloat16 [384, 128, 2048], P('orb', 'aux')
Inputs may be any that keep to these rules, and one draw needn't show every extreme that they name: partners[i, 0] = i for every orbital i; the other partners of an orbital are any orbitals, repeats allowed. `tile_pos`: the listed positions (row block, column block) are all distinct, and each of the 16 diagonal positions is listed.
All inputs are finite; a program needn't handle non-finite values.
Results may differ from a plain program's by a relative error of at most 0.0049.
Values may be sent and summed in bfloat16 or wider, within the bound.
A program may use at most 128 MiB of HBM per device.

v0:
```python
import jax
import jax.numpy as jnp
from jax import lax
from jax.sharding import PartitionSpec as P


def placed_terms(tile_set, positions, block_count):
    levels = jnp.arange(block_count, dtype=jnp.int32)
    row_hits = (positions[:, 0:1] == levels[None, :]).astype(jnp.bfloat16)
    col_hits = (positions[:, 1:2] == levels[None, :]).astype(jnp.bfloat16)
    pair_table = (row_hits[:, :, None] * col_hits[:, None, :]).reshape(
        tile_set.shape[0], block_count * block_count
    )
    flat_tiles = tile_set.reshape(tile_set.shape[0], tile_set.shape[1] * tile_set.shape[2])
    return lax.dot_general(
        pair_table, flat_tiles, (((0,), (0,)), ((), ())), preferred_element_type=jnp.float32
    )


def apply_metric(row_block, placed, block_count, span):
    blocks = placed.astype(jnp.bfloat16).reshape(block_count, block_count, span, span)
    rows_split = row_block.reshape(row_block.shape[0], block_count, span)
    result = jnp.einsum("ars,rcsu->acu", rows_split, blocks, preferred_element_type=jnp.float32)
    return result.reshape(row_block.shape[0], block_count * span)


def shards(factors, amplitudes, partners, metric_tiles, tile_pos):
    group_size, domain, aux_part = factors.shape
    flat_factors = factors.reshape(group_size, domain * aux_part)
    gathered = lax.all_gather(flat_factors, "orb", axis=0, tiled=True)
    picked = jnp.take(gathered, partners.reshape(-1), axis=0)
    picked = picked.reshape(partners.shape[0], partners.shape[1], domain, aux_part)
    gammas = jnp.einsum("ikab,ikbp->iap", amplitudes, picked, preferred_element_type=jnp.float32)
    gammas = gammas.astype(jnp.bfloat16)
    owned_rows = lax.all_to_all(gammas, "aux", split_axis=1, concat_axis=2, tiled=True)
    row_block = owned_rows.reshape(owned_rows.shape[0] * owned_rows.shape[1], owned_rows.shape[2])
    span = metric_tiles.shape[1]
    block_count = row_block.shape[1] // span
    placed = placed_terms(
        lax.all_gather(metric_tiles, "aux", axis=0, tiled=True),
        lax.all_gather(tile_pos, "aux", axis=0, tiled=True),
        block_count,
    )
    result = apply_metric(row_block, placed, block_count, span)
    return result.reshape(owned_rows.shape).astype(jnp.bfloat16)


def solution(mesh):
    in_specs = (
        P("orb", None, "aux"),
        P("orb", None, None, None),
        P("orb", None),
        P("aux", None, None),
        P("aux", None),
    )
    out_specs = P("orb", "aux", None)
    return jax.shard_map(shards, mesh=mesh, in_specs=in_specs, out_specs=out_specs, check_vma=False)
```

profile of v0, /device:TPU:24, one launch (start us, length us, event | category | flops | bytes accessed | tf_op | source)
XLA Modules:
  0.0 204.2 jit_solution(7695285728470506883)
XLA Ops:
  6.5 0.0 all-gather.4.cloned.1.call-start
  6.5 1.8 copy.22
  8.3 2.1 %reshape.111 = bf16[48,8192]{1,0:T(8,128)(2,1)} reshape(bf16[48,128,64]{2,1,0:T(8,128)(2,1)S(1)} %copy.22) | data formatting | bytes 1572864 | tf_op jit(solution)/shard_map/reshape | solution.py:29
  10.4 0.0 all-gather.4.cloned.1.call-update
  10.4 0.0 all-gather.6.cloned.1.call-start
  10.4 0.7 all-gather.6.cloned.1.call-update
  11.2 46.1 %all-gather = s32[32,4,2]{1,2,0:T(2,128)S(1)} all-gather(s32[1,4,2]{1,2,0:T(2,128)} %bitcast.51), channel_id=1, replica_groups=mesh['orb'=8,'aux'=32] {'aux'}, dimensions={0}, use_global_device_ids=true | all-gather | bytes 1056 | tf_op jit(solution)/shard_map/all_gather | solution.py:41
  57.2 0.1 reshape.124
  57.3 0.8 copy.23
  58.1 0.1 reshape.112
  58.2 0.7 compare_and_fusion
  58.9 0.1 copy.21
  59.1 0.0 all-gather.4.cloned.1.call-done
  59.1 24.6 %gather_fusion = bf16[576,8192]{1,0:T(8,128)(2,1)} fusion(bf16[384,8192]{1,0:T(8,128)(2,1)} %all-gather.4.cloned.1.call-done, s32[1024]{0:T(1024)S(1)} %pad_clamp_fusion), kind=kCustom, calls=%fused_computation | custom fusion | bytes 18876672 | tf_op jit(solution)/shard_map/jit(_take)/gather | solution.py:31
  83.7 26.1 %gather.7 = bf16[48,12,128,64]{3,2,1,0:T(8,128)(2,1)} reshape(bf16[576,8192]{1,0:T(8,128)(2,1)} %gather_fusion) | data formatting | bytes 18874368 | tf_op jit(solution)/shard_map/jit(_take)/gather | solution.py:31
  109.9 14.9 %fusion.10 = bf16[48,128,64]{1,2,0:T(8,128)(2,1)S(1)} fusion(bf16[48,12,128,128]{3,2,1,0:T(8,128)(2,1)} %param.6, bf16[48,12,128,64]{3,2,1,0:T(8,128)(2,1)} %gather.7, pred[48,12]{1,0:T(8,128)(4,1)S(1)} %copy.21), kind=kOutput, calls=%fused_computation.13 | convolution fusion | flops 1213071360 | bytes 29098560 | tf_op jit(solution)/shard_map/ikab,ikbp->iap/dot_general | solution.py:33
  124.7 1.0 copy.25
  125.7 1.9 reshape.129
  127.6 6.6 %all-to-all-start = ((bf16[32,2,6144]{2,1,0:T(2,128)(2,1)}), bf16[32,2,6144]{2,1,0:T(2,128)(2,1)S(1)}, u32[]{:S(2)}, u32[]{:S(2)}) async-start(bf16[32,2,6144]{2,1,0:T(2,128)(2,1)} %reshape.129), calls=%async_computation | async-start | bytes 1572864 | tf_op jit(solution)/shard_map/all_to_all | solution.py:35
  134.2 11.8 %all-gather.6.cloned.1.call-done = bf16[128,128,128]{2,1,0:T(8,128)(2,1)} async-done(((bf16[4,128,128]{2,1,0:T(8,128)(2,1)}), bf16[128,128,128]{2,1,0:T(8,128)(2,1)}) %all-gather.6.cloned.1.call-update) | async-done | bytes 4194320 | tf_op jit(solution)/shard_map/all_gather | solution.py:40
  146.1 8.8 %fusion.4 = bf16[32,8,128,128]{3,1,2,0:T(8,128)(2,1)} fusion(bf16[128,256]{0,1:T(8,128)(2,1)S(1)} %bitcast.50, bf16[16,8,128,128]{3,2,1,0:T(8,128)(2,1)} %bitcast.49), kind=kOutput, calls=%fused_computation.7 | convolution fusion | flops 1077936128 | bytes 12648448 | tf_op jit(solution)/shard_map/dot_general | solution.py:15
  154.9 9.2 %copy.35 = bf16[32,8,128,128]{3,2,1,0:T(8,128)(2,1)} copy(bf16[32,8,128,128]{3,1,2,0:T(8,128)(2,1)} %fusion.4) | data formatting | bytes 16777216
  164.1 10.4 %bitcast_bitcast_fusion = bf16[16,128,16,128]{1,3,0,2:T(8,128)(2,1)} fusion(bf16[16,16,128,128]{3,2,1,0:T(8,128)(2,1)} %bitcast.45), kind=kLoop, calls=%fused_computation.6 | loop fusion | bytes 16777216 | tf_op jit(solution)/shard_map/ars,rcsu->acu/dot_general | solution.py:23
  174.4 12.3 %copy.28 = bf16[16,128,16,128]{3,1,0,2:T(8,128)(2,1)} copy(bf16[16,128,16,128]{1,3,0,2:T(8,128)(2,1)} %bitcast_bitcast_fusion) | data formatting | bytes 16777216 | tf_op jit(solution)/shard_map/ars,rcsu->acu/dot_general | solution.py:23
  186.7 0.0 all-to-all-done
  186.8 1.0 reshape.130
  187.8 1.0 copy.26
  188.8 0.7 dot_general.16
  189.5 6.3 %fusion.7 = bf16[48,4,2048]{2,0,1:T(8,128)(2,1)S(1)} fusion(bf16[2048,16,128,1]{2,0,1,3:T(8,128)(2,1)} %bitcast.46, bf16[48,4,16,128]{3,2,1,0:T(8,128)(2,1)S(1)} %dot_general.16), kind=kOutput, calls=%fused_computation.11 | convolution fusion | flops 1611005952 | bytes 9961472 | tf_op jit(solution)/shard_map/ars,rcsu->acu/dot_general | solution.py:23
  195.9 1.5 copy.30
  (6 shorter events, 0.0 us)
Async XLA Ops:
  6.5 52.6 %all-gather.4.cloned.1.call-start = ((), (), s32[]{:S(2)}) async-start(), calls=%async_computation.1 | async-start | bytes 7077888 | tf_op jit(solution)/shard_map/all_gather | solution.py:30
  10.4 135.7 %all-gather.6.cloned.1.call-start = ((), (), s32[]{:S(2)}) async-start(), calls=%async_computation.2 | async-start | bytes 4325376 | tf_op jit(solution)/shard_map/all_gather | solution.py:40
  127.6 59.2 %all-to-all-start = ((bf16[32,2,6144]{2,1,0:T(2,128)(2,1)}), bf16[32,2,6144]{2,1,0:T(2,128)(2,1)S(1)}, u32[]{:S(2)}, u32[]{:S(2)}) async-start(bf16[32,2,6144]{2,1,0:T(2,128)(2,1)} %reshape.129), calls=%async_computation | async-start | bytes 1572864 | tf_op jit(solution)/shard_map/all_to_all | solution.py:35
Sparse Core Ops, SparseCore 0:
  10.5 44.1 all-gather.3
  57.4 88.6 all-gather.5
where the time goes:
time: 206 us; the launch traced here: 204 us
  local copies, waits for them, and re-layouts  94.6 us (46%)
  blocking collectives  46.1 us (22%)
  matrix products  30 us (15%)
  between operations  13.5 us (7%)
  waiting for transfers between devices  12.6 us (6%)
  starting transfers between devices  6.66 us (3%)
    gather x2, local copies, waits for them, and re-layouts, shards(): picked = jnp.take(gathered, partners.reshape(-1), axis=0)  50.7 us
    all_gather x1, blocking collectives, shards(): lax.all_gather(tile_pos, 'aux', axis=0, tiled=True)  46.1 us
    dot_general x3, local copies, waits for them, and re-layouts, apply_metric(): jnp.einsum('ars,rcsu->acu', rows_split, blocks, preferred_element_type=jn...  23.4 us
    dot_general x1, matrix products, shards(): jnp.einsum('ikab,ikbp->iap', amplitudes, picked, preferred_element_type=j...  14.9 us
    unnamed x6, local copies, waits for them, and re-layouts  14.7 us
    all_gather x1, waiting for transfers between devices, shards(): lax.all_gather(metric_tiles, 'aux', axis=0, tiled=True)  11.8 us
    dot_general x1, matrix products, placed_terms(): lax.dot_general(pair_table, flat_tiles, (((0,), (0,)), ((), ())), preferr...  8.82 us
    all_to_all x1, starting transfers between devices, shards(): lax.all_to_all(gammas, 'aux', split_axis=1, concat_axis=2, tiled=True)  6.62 us
  transfers between devices with their start and end apart: 3, of which 1 were waited for; matrix products, arithmetic and copies ran while one was open for 54% of the time, Pallas kernels for 0%

commit v1 on v0

--- a/solution.py
+++ b/solution.py
@@ -37,7 +37,9 @@
     span = metric_tiles.shape[1]
     block_count = row_block.shape[1] // span
     placed = placed_terms(
-        lax.all_gather(metric_tiles, "aux", axis=0, tiled=True),
+        jnp.concatenate(
+            lax.all_to_all(jnp.stack(lax.axis_size("aux") * [metric_tiles]), "aux", 0, 0), axis=0
+        ),
         lax.all_gather(tile_pos, "aux", axis=0, tiled=True),
         block_count,
     )

time: 206 us -> 289 us (1.40)
  blocking collectives: 46.1 us -> 128 us
  waiting for transfers between devices: 12.6 us -> 0.04 us
  starting transfers between devices: 6.66 us -> 18.4 us
  local copies, waits for them, and re-layouts: 94.6 us -> 97.9 us
    all_gather x1, blocking collectives: 46.1 us -> 128 us  [shards(): lax.all_gather(tile_pos, 'aux', axis=0, tiled=True)]
    all_gather x1 -> x0, waiting for transfers between devices: 11.8 us -> none  [shards(): lax.all_gather(metric_tiles, 'aux', axis=0, tiled=True)]
    all_to_all x0 -> x1, starting transfers between devices: none -> 11.4 us  [shards(): lax.all_to_all(jnp.stack(lax.axis_size('aux') * [metric_tiles]), 'aux', 0...]
    another operation x0 -> x1, local copies, waits for them, and re-layouts: none -> 3.93 us  [shards(): jnp.stack(lax.axis_size('aux') * [metric_tiles])]
    unnamed x6 -> x10, local copies, waits for them, and re-layouts: 14.7 us -> 14.1 us
  transfers between devices with their start and end apart: 3 -> 3, of which waited for: 1 -> 0; matrix products, arithmetic and copies ran while one was open for 54% -> 39% of each run, Pallas kernels for 0% -> 0%
where the time goes in v1:
time: 289 us; the launch traced here: 288 us
  blocking collectives  128 us (44%)
  local copies, waits for them, and re-layouts  97.9 us (34%)
  matrix products  29.7 us (10%)
  starting transfers between devices  18.4 us (6%)
  between operations  13.5 us (5%)
    all_gather x1, blocking collectives, shards(): lax.all_gather(tile_pos, 'aux', axis=0, tiled=True)  128 us
    gather x2, local copies, waits for them, and re-layouts, shards(): picked = jnp.take(gathered, partners.reshape(-1), axis=0)  50.7 us
    dot_general x3, local copies, waits for them, and re-layouts, apply_metric(): jnp.einsum('ars,rcsu->acu', rows_split, blocks, preferred_element_type=jn...  23.4 us
    dot_general x1, matrix products, shards(): jnp.einsum('ikab,ikbp->iap', amplitudes, picked, preferred_element_type=j...  14.6 us
    unnamed x10, local copies, waits for them, and re-layouts  14.1 us
    all_to_all x1, starting transfers between devices, shards(): lax.all_to_all(jnp.stack(lax.axis_size('aux') * [metric_tiles]), 'aux', 0...  11.4 us
    dot_general x1, matrix products, placed_terms(): lax.dot_general(pair_table, flat_tiles, (((0,), (0,)), ((), ())), preferr...  8.8 us
    all_to_all x1, starting transfers between devices, shards(): lax.all_to_all(gammas, 'aux', split_axis=1, concat_axis=2, tiled=True)  6.99 us
  transfers between devices with their start and end apart: 3, of which 0 were waited for; matrix products, arithmetic and copies ran while one was open for 39% of the time, Pallas kernels for 0%

profile of v1, /device:TPU:24, one launch (start us, length us, event | category | flops | bytes accessed | tf_op | source)
XLA Modules:
  0.0 287.6 jit_solution(15477783738014289195)
XLA Ops:
  6.5 0.0 all-gather.3.cloned.1.call-start
  6.5 1.8 copy.22
  8.3 0.0 copy-start.1
  8.3 0.0 copy-start
  8.3 2.1 reshape.110
  10.4 0.0 all-gather.3.cloned.1.call-update
  10.4 3.9 %stack.2 = bf16[32,4,128,128]{3,2,1,0:T(8,128)(2,1)} broadcast(bf16[4,128,128]{2,1,0:T(8,128)(2,1)} %param.8), dimensions={1,2,3} | broadcast | bytes 4325376 | tf_op jit(solution)/shard_map/stack | solution.py:41
  14.4 11.4 %all-to-all-start.1 = ((bf16[32,4,128,128]{3,2,1,0:T(8,128)(2,1)}), bf16[32,4,128,128]{3,2,1,0:T(8,128)(2,1)}, u32[]{:S(2)}, u32[]{:S(2)}) async-start(bf16[32,4,128,128]{3,2,1,0:T(8,128)(2,1)} %stack.2), calls=%async_computation.1 | async-start | bytes 8388608 | tf_op jit(solution)/shard_map/all_to_all | solution.py:41
  25.8 0.0 copy-done.1
  25.8 127.9 %all-gather = s32[32,4,2]{1,2,0:T(2,128)S(1)} all-gather(s32[1,4,2]{1,2,0:T(2,128)S(1)} %bitcast.51), channel_id=1, replica_groups=mesh['orb'=8,'aux'=32] {'aux'}, dimensions={0}, use_global_device_ids=true | all-gather | bytes 1056 | tf_op jit(solution)/shard_map/all_gather | solution.py:43
  153.8 0.1 reshape.122
  153.9 0.0 copy-done
  153.9 0.1 copy.23
  154.0 0.1 reshape.111
  154.1 0.1 copy.21
  154.3 0.0 all-gather.3.cloned.1.call-done
  154.3 24.6 %gather_fusion = bf16[576,8192]{1,0:T(8,128)(2,1)} fusion(bf16[384,8192]{1,0:T(8,128)(2,1)} %all-gather.3.cloned.1.call-done, s32[1024]{0:T(1024)S(1)} %pad_clamp_fusion), kind=kCustom, calls=%fused_computation | custom fusion | bytes 18876672 | tf_op jit(solution)/shard_map/jit(_take)/gather | solution.py:31
  178.9 26.1 %gather.7 = bf16[48,12,128,64]{3,2,1,0:T(8,128)(2,1)} reshape(bf16[576,8192]{1,0:T(8,128)(2,1)} %gather_fusion) | data formatting | bytes 18874368 | tf_op jit(solution)/shard_map/jit(_take)/gather | solution.py:31
  205.0 14.6 %fusion.10 = bf16[48,128,64]{1,2,0:T(8,128)(2,1)S(1)} fusion(bf16[48,12,128,128]{3,2,1,0:T(8,128)(2,1)} %param.6, bf16[48,12,128,64]{3,2,1,0:T(8,128)(2,1)} %gather.7, pred[48,12]{1,0:T(8,128)(4,1)S(1)} %copy.21), kind=kOutput, calls=%fused_computation.13 | convolution fusion | flops 1213071360 | bytes 29098560 | tf_op jit(solution)/shard_map/ikab,ikbp->iap/dot_general | solution.py:33
  219.6 1.0 copy.25
  220.6 1.9 reshape.127
  222.5 0.0 all-to-all-done.1
  222.5 7.0 %all-to-all-start = ((bf16[32,2,6144]{2,1,0:T(2,128)(2,1)}), bf16[32,2,6144]{2,1,0:T(2,128)(2,1)S(1)}, u32[]{:S(2)}, u32[]{:S(2)}) async-start(bf16[32,2,6144]{2,1,0:T(2,128)(2,1)} %reshape.127), calls=%async_computation | async-start | bytes 1572864 | tf_op jit(solution)/shard_map/all_to_all | solution.py:35
  229.5 8.8 %fusion.4 = bf16[32,8,128,128]{3,1,2,0:T(8,128)(2,1)} fusion(bf16[128,256]{0,1:T(8,128)(2,1)S(1)} %bitcast.50, bf16[16,8,128,128]{3,2,1,0:T(8,128)(2,1)} %bitcast.19), kind=kOutput, calls=%fused_computation.7 | convolution fusion | flops 1077936128 | bytes 12648448 | tf_op jit(solution)/shard_map/dot_general | solution.py:15
  238.3 9.2 %copy.35 = bf16[32,8,128,128]{3,2,1,0:T(8,128)(2,1)} copy(bf16[32,8,128,128]{3,1,2,0:T(8,128)(2,1)} %fusion.4) | data formatting | bytes 16777216
  247.5 10.3 %bitcast_bitcast_fusion = bf16[16,128,16,128]{1,3,0,2:T(8,128)(2,1)} fusion(bf16[16,16,128,128]{3,2,1,0:T(8,128)(2,1)} %bitcast.46), kind=kLoop, calls=%fused_computation.6 | loop fusion | bytes 16777216 | tf_op jit(solution)/shard_map/ars,rcsu->acu/dot_general | solution.py:23
  257.9 12.3 %copy.28 = bf16[16,128,16,128]{3,1,0,2:T(8,128)(2,1)} copy(bf16[16,128,16,128]{1,3,0,2:T(8,128)(2,1)} %bitcast_bitcast_fusion) | data formatting | bytes 16777216 | tf_op jit(solution)/shard_map/ars,rcsu->acu/dot_general | solution.py:23
  270.2 0.0 all-to-all-done
  270.2 1.0 reshape.128
  271.2 1.0 copy.26
  272.2 0.7 dot_general.16
  273.0 6.3 %fusion.7 = bf16[48,4,2048]{2,0,1:T(8,128)(2,1)S(1)} fusion(bf16[2048,16,128,1]{2,0,1,3:T(8,128)(2,1)} %bitcast.47, bf16[48,4,16,128]{3,2,1,0:T(8,128)(2,1)S(1)} %dot_general.16), kind=kOutput, calls=%fused_computation.11 | convolution fusion | flops 1611005952 | bytes 9961472 | tf_op jit(solution)/shard_map/ars,rcsu->acu/dot_general | solution.py:23
  279.3 1.5 copy.30
  (7 shorter events, 0.1 us)
Async XLA Ops:
  6.5 147.8 %all-gather.3.cloned.1.call-start = ((), (), s32[]{:S(2)}) async-start(), calls=%async_computation.2 | async-start | bytes 7077888 | tf_op jit(solution)/shard_map/all_gather | solution.py:30
  8.3 17.5 %copy-start.1 = (s32[4,2]{0,1:T(2,128)S(1)}, s32[4,2]{0,1:T(2,128)}, u32[]{:S(2)}) copy-start(s32[4,2]{0,1:T(2,128)} %param.9) | copy-start | bytes 100
  8.3 145.6 %copy-start = (s32[48,12]{0,1:T(8,128)S(1)}, s32[48,12]{0,1:T(8,128)}, u32[]{:S(2)}) copy-start(s32[48,12]{0,1:T(8,128)} %param.7) | copy-start | bytes 6916
  14.4 208.1 %all-to-all-start.1 = ((bf16[32,4,128,128]{3,2,1,0:T(8,128)(2,1)}), bf16[32,4,128,128]{3,2,1,0:T(8,128)(2,1)}, u32[]{:S(2)}, u32[]{:S(2)}) async-start(bf16[32,4,128,128]{3,2,1,0:T(8,128)(2,1)} %stack.2), calls=%async_computation.1 | async-start | bytes 8388608 | tf_op jit(solution)/shard_map/all_to_all | solution.py:41
  222.5 47.7 %all-to-all-start = ((bf16[32,2,6144]{2,1,0:T(2,128)(2,1)}), bf16[32,2,6144]{2,1,0:T(2,128)(2,1)S(1)}, u32[]{:S(2)}, u32[]{:S(2)}) async-start(bf16[32,2,6144]{2,1,0:T(2,128)(2,1)} %reshape.127), calls=%async_computation | async-start | bytes 1572864 | tf_op jit(solution)/shard_map/all_to_all | solution.py:35
Sparse Core Ops, SparseCore 0:
  10.5 44.1 all-gather.2
